TPU v7x, 32 devices: a whole 2x2x4 slice. The times are simulated.
32 devices in a mesh: day: 2 (over y), stu: 16 (over z, x, core).
Axes of the slice: x: 2, y: 2, z: 4, core: 2. Of those that a mesh axis runs over, the one named last changes fastest.
Arguments:
- performance: bfloat16 [64, 128, 1024], P('day', 'stu'), may hold values from -8 to 8
- student_factor: bfloat16 [128, 256], P('stu'), may hold values from -0.5 to 0.5
- skill_factor: bfloat16 [1024, 256], replicated, may hold values from -0.1875 to 0.1875
- day_prev: float32 [64, 256], P('day'), may hold values from -6 to 6
- ar_coef: float32 [7], replicated, may hold values from -0.3 to 0.3
Outputs:
- day_factor: float32 [64, 256], P('day', 'stu')
- residual: float32 [64, 256], P('day', 'stu')
All inputs are finite; a program needn't handle non-finite values.
Results may differ from a plain program's by a relative error of at most 0.0003.
Values sent between devices are 32-bit elements; how exact they have to be, the bound alone decides.
No kernel may reach another device: no remote copies, remote signals or barrier semaphores. Data moves between devices by JAX's collectives and lax.ppermute only.
A program may use at most 64 MiB of HBM per device.

v0:
```python
import jax
import jax.numpy as jnp
from jax import lax
from jax.sharding import PartitionSpec as P

LAGS = 7
ITERS = 3
smoothing = 1.0


def shifted(block, axis, distance):
    devices = range(lax.axis_size(axis))
    route = [(i - distance, i) for i in devices if i - distance in devices]
    return lax.ppermute(block, axis, route)


def filter_rows(extended, coef, count):
    out = extended[LAGS : LAGS + count]
    for lag in range(1, LAGS + 1):
        out = out - coef[lag - 1] * extended[LAGS - lag : LAGS - lag + count]
    return out


def smooth(values, coef):
    count = values.shape[0]
    below = shifted(values[count - LAGS :], "day", 1)
    ahead_core = filter_rows(jnp.concatenate([below, values], 0), coef, count)
    above = shifted(ahead_core[:LAGS], "day", -1)
    ahead = jnp.concatenate([ahead_core, above], 0)
    out = ahead[:count]
    for lag in range(1, LAGS + 1):
        out = out - coef[lag - 1] * ahead[lag : lag + count]
    return out


def with_gram(values, gram_part):
    return jnp.dot(
        lax.all_gather(values, "stu", axis=1, tiled=True),
        gram_part,
        precision=lax.Precision.HIGHEST,
        preferred_element_type=jnp.float32,
    )


def operate(values, gram_part, coef):
    return with_gram(values, gram_part) + smoothing * smooth(values, coef)


def global_total(value):
    return lax.psum(value, ("day", "stu"))


def summed_gram(local_gram):
    return lax.psum(local_gram, "stu")


def local(performance, student_factor, skill_factor, day_prev, ar_coef):
    days, students, skills = performance.shape
    rank = skill_factor.shape[1]
    proj = jnp.dot(
        performance.reshape(days * students, skills),
        skill_factor,
        preferred_element_type=jnp.float32,
    )
    proj = proj.reshape(days, students, rank)
    local_terms = jnp.sum(proj * student_factor.astype(jnp.float32)[None], axis=1)
    local_gram = jnp.dot(student_factor.T, student_factor, preferred_element_type=jnp.float32)
    skill_gram = jnp.dot(skill_factor.T, skill_factor, preferred_element_type=jnp.float32)
    columns = rank // lax.axis_size("stu")
    first_col = lax.axis_index("stu") * columns
    gram = summed_gram(local_gram) * skill_gram
    mttkrp = lax.psum_scatter(local_terms, "stu", scatter_dimension=1, tiled=True)
    gram_part = lax.dynamic_slice_in_dim(gram, first_col, columns, 1)
    day_factor = lax.dynamic_slice_in_dim(day_prev, first_col, columns, 1)
    residual = mttkrp - operate(day_factor, gram_part, ar_coef)
    direction = residual
    norm_now = global_total(jnp.sum(residual * residual))
    for step in range(ITERS):
        image = operate(direction, gram_part, ar_coef)
        alpha = norm_now / global_total(jnp.sum(direction * image))
        day_factor = day_factor + alpha * direction
        residual = residual - alpha * image
        norm_next = global_total(jnp.sum(residual * residual))
        direction = residual + norm_next / norm_now * direction
        norm_now = norm_next
    return (day_factor, residual)


def solution(mesh):
    return jax.shard_map(
        local,
        mesh=mesh,
        in_specs=(P("day", "stu", None), P("stu", None), P(), P("day", None), P()),
        out_specs=(P("day", "stu"), P("day", "stu")),
        check_vma=False,
    )
```

profile of v0, /device:TPU:14, one launch (start us, length us, event | category | flops | bytes accessed | tf_op | source)
XLA Modules:
  0.0 491.8 jit_solution(908321572501885240)
XLA Ops:
  9.6 1.7 fusion.139
  14.3 15.5 %all_gather.12 = f32[32,256]{0,1:T(8,128)S(1)} all-gather(f32[32,16]{0,1:T(8,128)S(1)} %copy.10), channel_id=1, replica_groups=mesh['day'=2,'stu'=16] {'stu'}, dimensions={1}, use_global_device_ids=true | all-gather | bytes 34816 | tf_op jit(solution)/shard_map/all_gather | solution.py:38
  29.8 4.5 fusion.120
  34.3 4.6 collective-permute-start.1
  38.9 64.2 %all-reduce.3.cloned.1.call-done = f32[256,256]{0,1:T(8,128)} async-done(((f32[256,256]{0,1:T(8,128)}), f32[256,256]{0,1:T(8,128)}) %all-reduce.3.cloned.1.call-update) | async-done | bytes 262160 | tf_op jit(solution)/shard_map/psum | solution.py:54
  103.8 57.7 %reduce-scatter.2.cloned.1.call-done = f32[32,16]{0,1:T(8,128)} async-done(((f32[32,256]{0,1:T(8,128)}), f32[32,16]{0,1:T(8,128)}) %reduce-scatter.2.cloned.1.call-update) | async-done | bytes 2064 | tf_op jit(solution)/shard_map/reduce_scatter | solution.py:72
  161.5 5.2 %fusion.104 = f32[32,16]{0,1:T(8,128)S(1)} fusion(f32[32,16]{0,1:T(8,128)} %reduce-scatter.2.cloned.1.call-done, f32[7,16]{0,1:T(8,128)S(1)} %collective-permute-done.1, f32[32,16]{0,1:T(8,128)S(1)} %fusion.120, f32[]{:T(128)} %bitcast.7, f32[]{:T(128)} %bitcast.6, f32[]{:T(128)} %bitcast.5, f32[]{:T(128)} %bitcast.4, f32[]{:T(128)} %bitcast.3, ...), kind=kOutput, calls=%fused_computation.173 | convolution fusion | flops 1584640 | bytes 55772 | tf_op jit(solution)/shard_map/dot_general | solution.py:37
  168.1 4.2 collective-permute-done.2
  172.3 4.5 fusion.86
  178.5 15.4 %all_gather.13 = f32[32,256]{0,1:T(8,128)S(1)} all-gather(f32[32,16]{0,1:T(8,128)S(1)} %fusion.104), channel_id=1, replica_groups=mesh['day'=2,'stu'=16] {'stu'}, dimensions={1}, use_global_device_ids=true | all-gather | bytes 34816 | tf_op jit(solution)/shard_map/all_gather | solution.py:38
  193.8 5.2 %multiply_reduce_fusion.4 = (f32[]{:T(128)}, f32[]{:T(128)}, f32[32,16]{0,1:T(8,128)S(1)}) fusion(f32[32,16]{0,1:T(8,128)S(1)} %fusion.104, f32[7,16]{0,1:T(8,128)S(1)} %collective-permute-done.3, f32[32,16]{0,1:T(8,128)S(1)} %fusion.86, f32[]{:T(128)} %bitcast.7, f32[]{:T(128)} %bitcast.6, f32[]{:T(128)} %bitcast.5, f32[]{:T(128)} %bitcast.4, ...), kind=kOutput, calls=%fused_computation.235 | convolution fusion | flops 1586174 | bytes 55780 | tf_op jit(solution)/shard_map/dot_general | solution.py:37
  199.0 44.1 %all-reduce = (f32[]{:T(128)}, f32[]{:T(128)}) all-reduce(f32[]{:T(128)} %get-tuple-element.3, f32[]{:T(128)} %get-tuple-element.2), channel_id=1, replica_groups=mesh['day'=2,'stu'=16] {'day','stu'}, use_global_device_ids=true, to_apply=%region_4.0 | all-reduce | flops 2 | bytes 16 | tf_op jit(solution)/shard_map/psum | solution.py:50
  245.1 38.6 %psum.52 = f32[]{:T(128)} all-reduce(f32[]{:T(128)} %multiply_reduce_fusion.3), channel_id=1, replica_groups=mesh['day'=2,'stu'=16] {'day','stu'}, use_global_device_ids=true, to_apply=%region_8.0 | all-reduce | flops 1 | bytes 8 | tf_op jit(solution)/shard_map/psum | solution.py:50
  286.4 4.2 collective-permute-done.4
  290.7 4.5 fusion.53
  296.8 18.0 %all_gather.14 = f32[32,256]{0,1:T(8,128)S(1)} all-gather(f32[32,16]{0,1:T(8,128)S(1)} %multiply_add_fusion.2), channel_id=1, replica_groups=mesh['day'=2,'stu'=16] {'stu'}, dimensions={1}, use_global_device_ids=true | all-gather | bytes 34816 | tf_op jit(solution)/shard_map/all_gather | solution.py:38
  314.8 5.2 %multiply_reduce_fusion.2 = (f32[]{:T(128)}, f32[32,16]{0,1:T(8,128)S(1)}) fusion(f32[32,16]{0,1:T(8,128)S(1)} %multiply_add_fusion.2, f32[7,16]{0,1:T(8,128)S(1)} %collective-permute-done.5, f32[32,16]{0,1:T(8,128)S(1)} %fusion.53, f32[]{:T(128)} %bitcast.7, f32[]{:T(128)} %bitcast.6, f32[]{:T(128)} %bitcast.5, f32[]{:T(128)} %bitcast.4, f32[]{:T(128)} %bitcast.3, ...), kind=kOutput, calls=%fused_computation.231 | convolution fusion | flops 1585151 | bytes 55776 | tf_op jit(solution)/shard_map/dot_general | solution.py:37
  320.0 43.0 %psum.53 = f32[]{:T(128)} all-reduce(f32[]{:T(128)} %get-tuple-element.10), channel_id=1, replica_groups=mesh['day'=2,'stu'=16] {'day','stu'}, use_global_device_ids=true, to_apply=%region_10.0 | all-reduce | flops 1 | bytes 8 | tf_op jit(solution)/shard_map/psum | solution.py:50
  364.8 39.0 %psum.54 = f32[]{:T(128)} all-reduce(f32[]{:T(128)} %get-tuple-element.8), channel_id=1, replica_groups=mesh['day'=2,'stu'=16] {'day','stu'}, use_global_device_ids=true, to_apply=%region_12.0 | all-reduce | flops 1 | bytes 8 | tf_op jit(solution)/shard_map/psum | solution.py:50
  406.5 4.2 collective-permute-done.6
  410.8 4.5 fusion.20
  416.9 17.6 %all_gather.15 = f32[32,256]{0,1:T(8,128)S(1)} all-gather(f32[32,16]{0,1:T(8,128)S(1)} %multiply_add_fusion.1), channel_id=1, replica_groups=mesh['day'=2,'stu'=16] {'stu'}, dimensions={1}, use_global_device_ids=true | all-gather | bytes 34816 | tf_op jit(solution)/shard_map/all_gather | solution.py:38
  434.5 5.1 %multiply_reduce_fusion = (f32[]{:T(128)}, f32[32,16]{0,1:T(8,128)S(1)}) fusion(f32[32,16]{0,1:T(8,128)S(1)} %multiply_add_fusion.1, f32[7,16]{0,1:T(8,128)S(1)} %collective-permute-done.7, f32[32,16]{0,1:T(8,128)S(1)} %fusion.20, f32[]{:T(128)} %bitcast.7, f32[]{:T(128)} %bitcast.6, f32[]{:T(128)} %bitcast.5, f32[]{:T(128)} %bitcast.4, f32[]{:T(128)} %bitcast.3, ...), kind=kOutput, calls=%fused_computation.227 | convolution fusion | flops 1585151 | bytes 55776 | tf_op jit(solution)/shard_map/dot_general | solution.py:37
  439.7 43.2 %psum.55 = f32[]{:T(128)} all-reduce(f32[]{:T(128)} %get-tuple-element.6), channel_id=1, replica_groups=mesh['day'=2,'stu'=16] {'day','stu'}, use_global_device_ids=true, to_apply=%region_14.0 | all-reduce | flops 1 | bytes 8 | tf_op jit(solution)/shard_map/psum | solution.py:50
  (41 shorter events, 17.0 us)
Async XLA Ops:
  7.2 4.8 copy-start
  7.2 4.8 copy-start.1
  7.2 95.9 %all-reduce.3.cloned.1.call-start = ((), (), s32[]{:S(2)}) async-start(), calls=%async_computation.2 | async-start | bytes 524288 | tf_op jit(solution)/shard_map/psum | solution.py:54
  8.3 21.6 %collective-permute-start = (f32[7,16]{0,1:T(8,128)S(1)}, f32[7,16]{0,1:T(8,128)S(1)}, u32[]{:S(2)}, u32[]{:S(2)}) collective-permute-start(f32[7,16]{0,1:T(8,128)S(1)} %slice.333), channel_id=1, source_target_pairs={{0,16},{1,17},{2,18},{3,19},{4,20},{5,21},{6,22},{7,23},{8,24},{9,... | collective-permute-start | bytes 1352 | tf_op jit(solution)/shard_map/ppermute | solution.py:14
  11.2 0.7 copy-start.2
  11.3 150.2 %reduce-scatter.2.cloned.1.call-start = ((), (), s32[]{:S(2)}) async-start(), calls=%async_computation.1 | async-start | bytes 139264 | tf_op jit(solution)/shard_map/reduce_scatter | solution.py:72
  13.0 0.7 copy-start.3
  34.3 69.5 %collective-permute-start.1 = (f32[7,16]{0,1:T(8,128)S(1)}, f32[7,16]{0,1:T(8,128)S(1)}, u32[]{:S(2)}, u32[]{:S(2)}) collective-permute-start(f32[7,16]{0,1:T(8,128)S(1)} %bitcast.27), channel_id=1, source_target_pairs={{16,0},{17,1},{18,2},{19,3},{20,4},{21,5},{22,6},{23,7},{24,8},{25... | collective-permute-start | bytes 1352 | tf_op jit(solution)/shard_map/ppermute | solution.py:14
  166.8 5.5 %collective-permute-start.2 = (f32[7,16]{0,1:T(8,128)S(1)}, f32[7,16]{0,1:T(8,128)S(1)}, u32[]{:S(2)}, u32[]{:S(2)}) collective-permute-start(f32[7,16]{0,1:T(8,128)S(1)} %slice.359), channel_id=1, source_target_pairs={{0,16},{1,17},{2,18},{3,19},{4,20},{5,21},{6,22},{7,23},{8,24},{9,... | collective-permute-start | bytes 1352 | tf_op jit(solution)/shard_map/ppermute | solution.py:14
  176.8 17.0 %collective-permute-start.3 = (f32[7,16]{0,1:T(8,128)S(1)}, f32[7,16]{0,1:T(8,128)S(1)}, u32[]{:S(2)}, u32[]{:S(2)}) collective-permute-start(f32[7,16]{0,1:T(8,128)S(1)} %bitcast.29), channel_id=1, source_target_pairs={{16,0},{17,1},{18,2},{19,3},{20,4},{21,5},{22,6},{23,7},{24,8},{25... | collective-permute-start | bytes 1352 | tf_op jit(solution)/shard_map/ppermute | solution.py:14
  285.1 5.5 %collective-permute-start.4 = (f32[7,16]{0,1:T(8,128)S(1)}, f32[7,16]{0,1:T(8,128)S(1)}, u32[]{:S(2)}, u32[]{:S(2)}) collective-permute-start(f32[7,16]{0,1:T(8,128)S(1)} %slice.385), channel_id=1, source_target_pairs={{0,16},{1,17},{2,18},{3,19},{4,20},{5,21},{6,22},{7,23},{8,24},{9,... | collective-permute-start | bytes 1352 | tf_op jit(solution)/shard_map/ppermute | solution.py:14
  295.1 19.6 %collective-permute-start.5 = (f32[7,16]{0,1:T(8,128)S(1)}, f32[7,16]{0,1:T(8,128)S(1)}, u32[]{:S(2)}, u32[]{:S(2)}) collective-permute-start(f32[7,16]{0,1:T(8,128)S(1)} %bitcast.30), channel_id=1, source_target_pairs={{16,0},{17,1},{18,2},{19,3},{20,4},{21,5},{22,6},{23,7},{24,8},{25... | collective-permute-start | bytes 1352 | tf_op jit(solution)/shard_map/ppermute | solution.py:14
  405.3 5.5 %collective-permute-start.6 = (f32[7,16]{0,1:T(8,128)S(1)}, f32[7,16]{0,1:T(8,128)S(1)}, u32[]{:S(2)}, u32[]{:S(2)}) collective-permute-start(f32[7,16]{0,1:T(8,128)S(1)} %slice.411), channel_id=1, source_target_pairs={{0,16},{1,17},{2,18},{3,19},{4,20},{5,21},{6,22},{7,23},{8,24},{9,... | collective-permute-start | bytes 1352 | tf_op jit(solution)/shard_map/ppermute | solution.py:14
  415.3 19.3 %collective-permute-start.7 = (f32[7,16]{0,1:T(8,128)S(1)}, f32[7,16]{0,1:T(8,128)S(1)}, u32[]{:S(2)}, u32[]{:S(2)}) collective-permute-start(f32[7,16]{0,1:T(8,128)S(1)} %bitcast.28), channel_id=1, source_target_pairs={{16,0},{17,1},{18,2},{19,3},{20,4},{21,5},{22,6},{23,7},{24,8},{25... | collective-permute-start | bytes 1352 | tf_op jit(solution)/shard_map/ppermute | solution.py:14
Sparse Core Ops, SparseCore 0:
  11.4 91.6 all-reduce.2
  106.5 54.8 reduce-scatter.1
where the time goes:
time: 494 us; the launch traced here: 492 us
  blocking collectives  274 us (55%)
  waiting for transfers between devices  135 us (27%)
  matrix products  23.1 us (5%)
  between operations  20.9 us (4%)
  other arithmetic  20.4 us (4%)
  starting transfers between devices  14.7 us (3%)
    psum x5, blocking collectives, global_total(): return lax.psum(value, ('day', 'stu'))  208 us
    all_gather x4, blocking collectives, with_gram(): lax.all_gather(values, 'stu', axis=1, tiled=True)  66.5 us
    psum x1, waiting for transfers between devices, summed_gram(): return lax.psum(local_gram, 'stu')  64.2 us
    reduce_scatter x1, waiting for transfers between devices, local(): lax.psum_scatter(local_terms, 'stu', scatter_dimension=1, tiled=True)  57.7 us
    dot_general x4, matrix products, with_gram(): jnp.dot(lax.all_gather(values, 'stu', axis=1, tiled=True), gram_part, pre...  20.8 us
    sub x4, other arithmetic, filter_rows(): out = out - coef[lag - 1] * extended[LAGS - lag:LAGS - lag + count]  17.8 us
    ppermute x8, starting transfers between devices, shifted(): return lax.ppermute(block, axis, route)  14.6 us
    ppermute x8, waiting for transfers between devices, shifted(): return lax.ppermute(block, axis, route)  12.7 us
  transfers between devices with their start and end apart: 10, of which 5 were waited for; matrix products, arithmetic and copies ran while one was open for 2% of the time, Pallas kernels for 0%

commit v1 on v0

--- a/solution.py
+++ b/solution.py
@@ -1,3 +1,4 @@
+import functools
 import jax
 import jax.numpy as jnp
 from jax import lax
@@ -6,6 +7,22 @@
 LAGS = 7
 ITERS = 3
 smoothing = 1.0
+
+
+def read_hubs(arr, array_dim):
+    num = jax.lax.axis_size("stu")
+    chunks = [arr]
+    jj = 1
+    while jj < num:
+        clean = jax.lax.ppermute(chunks[jj - 1], "stu", [(u, (u - 1) % num) for u in range(num)])
+        chunks.append(clean)
+        jj += 1
+    z_new = jnp.concatenate(chunks, axis=array_dim)
+    reached = jax.lax.axis_index("stu")
+    return jnp.roll(z_new, reached * arr.shape[array_dim], axis=array_dim)
+
+
+write_stops_all_on_mesh = functools.partial(read_hubs, array_dim=1)
 
 
 def shifted(block, axis, distance):
@@ -35,7 +52,7 @@
 
 def with_gram(values, gram_part):
     return jnp.dot(
-        lax.all_gather(values, "stu", axis=1, tiled=True),
+        write_stops_all_on_mesh(values),
         gram_part,
         precision=lax.Precision.HIGHEST,
         preferred_element_type=jnp.float32,

time: 494 us -> 729 us (1.48)
  waiting for transfers between devices: 135 us -> 269 us
  starting transfers between devices: 14.7 us -> 114 us
    ppermute x0 -> x60, waiting for transfers between devices: none -> 132 us  [read_hubs(): jax.lax.ppermute(chunks[jj - 1], 'stu', [(u, (u - 1) % num) for u in rang...]
    ppermute x0 -> x60, starting transfers between devices: none -> 91.4 us  [read_hubs(): jax.lax.ppermute(chunks[jj - 1], 'stu', [(u, (u - 1) % num) for u in rang...]
    all_gather x4 -> x0, blocking collectives: 66.5 us -> none  [with_gram(): lax.all_gather(values, 'stu', axis=1, tiled=True)]
    psum x5, blocking collectives: 208 us -> 271 us  [global_total(): return lax.psum(value, ('day', 'stu'))]
    psum x1, waiting for transfers between devices: 64.2 us -> 78.9 us  [summed_gram(): return lax.psum(local_gram, 'stu')]
    ppermute x8, waiting for transfers between devices: 12.7 us -> 0.25 us  [shifted(): return lax.ppermute(block, axis, route)]
    ppermute x8, starting transfers between devices: 14.6 us -> 22.2 us  [shifted(): return lax.ppermute(block, axis, route)]
  transfers between devices with their start and end apart: 10 -> 70, of which waited for: 5 -> 58; matrix products, arithmetic and copies ran while one was open for 2% -> 4% of each run, Pallas kernels for 0% -> 0%
where the time goes in v1:
time: 729 us; the launch traced here: 725 us
  blocking collectives  271 us (37%)
  waiting for transfers between devices  269 us (37%)
  starting transfers between devices  114 us (16%)
  matrix products  22.8 us (3%)
  between operations  20.9 us (3%)
  other arithmetic  20.6 us (3%)
  local copies, waits for them, and re-layouts  7.9 us (1%)
    psum x5, blocking collectives, global_total(): return lax.psum(value, ('day', 'stu'))  271 us
    ppermute x60, waiting for transfers between devices, read_hubs(): jax.lax.ppermute(chunks[jj - 1], 'stu', [(u, (u - 1) % num) for u in rang...  132 us
    ppermute x60, starting transfers between devices, read_hubs(): jax.lax.ppermute(chunks[jj - 1], 'stu', [(u, (u - 1) % num) for u in rang...  91.4 us
    psum x1, waiting for transfers between devices, summed_gram(): return lax.psum(local_gram, 'stu')  78.9 us
    reduce_scatter x1, waiting for transfers between devices, local(): lax.psum_scatter(local_terms, 'stu', scatter_dimension=1, tiled=True)  57.7 us
    ppermute x8, starting transfers between devices, shifted(): return lax.ppermute(block, axis, route)  22.2 us
    dot_general x4, matrix products, with_gram(): jnp.dot(write_stops_all_on_mesh(values), gram_part, precision=lax.Precisi...  21.2 us
    sub x4, other arithmetic, filter_rows(): out = out - coef[lag - 1] * extended[LAGS - lag:LAGS - lag + count]  18 us
  transfers between devices with their start and end apart: 70, of which 58 were waited for; matrix products, arithmetic and copies ran while one was open for 4% of the time, Pallas kernels for 0%

profile of v1, /device:TPU:14, one launch (start us, length us, event | category | flops | bytes accessed | tf_op | source)
XLA Modules:
  0.0 725.5 jit_solution(4541474678584806756)
XLA Ops:
  52.4 4.7 collective-permute-start.12
  63.6 5.0 collective-permute-start.14
  68.7 4.5 fusion.142
  73.2 4.3 collective-permute-start.16
  78.7 78.9 %all-reduce.3.cloned.1.call-done = f32[256,256]{0,1:T(8,128)} async-done(((f32[256,256]{0,1:T(8,128)}), f32[256,256]{0,1:T(8,128)}) %all-reduce.3.cloned.1.call-update) | async-done | bytes 262160 | tf_op jit(solution)/shard_map/psum | solution.py:71
  158.3 57.7 %reduce-scatter.2.cloned.1.call-done = f32[32,16]{0,1:T(8,128)} async-done(((f32[32,256]{0,1:T(8,128)}), f32[32,16]{0,1:T(8,128)}) %reduce-scatter.2.cloned.1.call-update) | async-done | bytes 2064 | tf_op jit(solution)/shard_map/reduce_scatter | solution.py:89
  216.0 5.3 fusion.26
  272.9 4.9 collective-permute-start.31
  277.8 4.5 fusion.110
  282.3 4.3 collective-permute-start.33
  288.0 5.3 multiply_reduce_fusion.4
  293.3 62.6 %all-reduce = (f32[]{:T(128)}, f32[]{:T(128)}) all-reduce(f32[]{:T(128)} %get-tuple-element.4, f32[]{:T(128)} %get-tuple-element.3), channel_id=1, replica_groups=mesh['day'=2,'stu'=16] {'day','stu'}, use_global_device_ids=true, to_apply=%region_4.6 | all-reduce | flops 2 | bytes 16 | tf_op jit(solution)/shard_map/psum | solution.py:67
  357.7 40.3 %psum.52 = f32[]{:T(128)} all-reduce(f32[]{:T(128)} %multiply_reduce_fusion.3), channel_id=1, replica_groups=mesh['day'=2,'stu'=16] {'day','stu'}, use_global_device_ids=true, to_apply=%region_8.10 | all-reduce | flops 1 | bytes 8 | tf_op jit(solution)/shard_map/psum | solution.py:67
  446.4 4.4 collective-permute-start.47
  452.2 4.9 collective-permute-start.48
  457.2 4.5 fusion.78
  467.3 5.3 multiply_reduce_fusion.2
  472.6 63.7 %psum.53 = f32[]{:T(128)} all-reduce(f32[]{:T(128)} %get-tuple-element.17), channel_id=1, replica_groups=mesh['day'=2,'stu'=16] {'day','stu'}, use_global_device_ids=true, to_apply=%region_10.12 | all-reduce | flops 1 | bytes 8 | tf_op jit(solution)/shard_map/psum | solution.py:67
  538.3 40.3 %psum.54 = f32[]{:T(128)} all-reduce(f32[]{:T(128)} %get-tuple-element.7), channel_id=1, replica_groups=mesh['day'=2,'stu'=16] {'day','stu'}, use_global_device_ids=true, to_apply=%region_12.14 | all-reduce | flops 1 | bytes 8 | tf_op jit(solution)/shard_map/psum | solution.py:67
  626.8 4.4 collective-permute-start.64
  632.7 4.9 collective-permute-start.65
  637.6 4.5 fusion.46
  647.8 5.3 multiply_reduce_fusion
  653.0 63.7 %psum.55 = f32[]{:T(128)} all-reduce(f32[]{:T(128)} %get-tuple-element.19), channel_id=1, replica_groups=mesh['day'=2,'stu'=16] {'day','stu'}, use_global_device_ids=true, to_apply=%region_14.16 | all-reduce | flops 1 | bytes 8 | tf_op jit(solution)/shard_map/psum | solution.py:67
  (224 shorter events, 216.3 us)
Async XLA Ops:
  7.2 150.4 %all-reduce.3.cloned.1.call-start = ((), (), s32[]{:S(2)}) async-start(), calls=%async_computation.2 | async-start | bytes 524288 | tf_op jit(solution)/shard_map/psum | solution.py:71
  24.6 4.0 collective-permute-start.5
  32.5 4.0 collective-permute-start.7
  40.5 4.0 collective-permute-start.9
  40.6 28.1 %collective-permute-start.15 = (f32[7,16]{0,1:T(8,128)S(1)}, f32[7,16]{0,1:T(8,128)S(1)}, u32[]{:S(2)}, u32[]{:S(2)}) collective-permute-start(f32[7,16]{0,1:T(8,128)S(1)} %slice.333), channel_id=1, source_target_pairs={{0,16},{1,17},{2,18},{3,19},{4,20},{5,21},{6,22},{7,23},{8,24},{9,... | collective-permute-start | bytes 1352 | tf_op jit(solution)/shard_map/ppermute | solution.py:31
  46.2 169.8 %reduce-scatter.2.cloned.1.call-start = ((), (), s32[]{:S(2)}) async-start(), calls=%async_computation.1 | async-start | bytes 139264 | tf_op jit(solution)/shard_map/reduce_scatter | solution.py:89
  52.4 6.0 collective-permute-start.12
  58.5 5.2 collective-permute-start.13
  63.6 14.8 %collective-permute-start.14 = (f32[32,16]{0,1:T(8,128)S(1)}, f32[32,16]{0,1:T(8,128)S(1)}, u32[]{:S(2)}, u32[]{:S(2)}) collective-permute-start(f32[32,16]{0,1:T(8,128)S(1)} %collective-permute-done.13), channel_id=1, source_target_pairs={{0,15},{1,0},{2,1},{3,2},{4,3},{5,4},{6,5},{7,6},{8,7},{9,8},{10,9... | collective-permute-start | bytes 6152 | tf_op jit(solution)/shard_map/ppermute | solution.py:17
  73.2 85.1 %collective-permute-start.16 = (f32[7,16]{0,1:T(8,128)S(1)}, f32[7,16]{0,1:T(8,128)S(1)}, u32[]{:S(2)}, u32[]{:S(2)}) collective-permute-start(f32[7,16]{0,1:T(8,128)S(1)} %bitcast.23), channel_id=1, source_target_pairs={{16,0},{17,1},{18,2},{19,3},{20,4},{21,5},{22,6},{23,7},{24,8},{25... | collective-permute-start | bytes 1352 | tf_op jit(solution)/shard_map/ppermute | solution.py:31
  267.9 5.0 collective-permute-start.30
  271.5 6.3 collective-permute-start.32
  272.9 14.8 %collective-permute-start.31 = (f32[32,16]{0,1:T(8,128)S(1)}, f32[32,16]{0,1:T(8,128)S(1)}, u32[]{:S(2)}, u32[]{:S(2)}) collective-permute-start(f32[32,16]{0,1:T(8,128)S(1)} %collective-permute-done.30), channel_id=1, source_target_pairs={{0,15},{1,0},{2,1},{3,2},{4,3},{5,4},{6,5},{7,6},{8,7},{9,8},{10,9... | collective-permute-start | bytes 6152 | tf_op jit(solution)/shard_map/ppermute | solution.py:17
  282.3 5.6 collective-permute-start.33
  441.6 4.7 collective-permute-start.46
  446.4 5.8 collective-permute-start.47
  450.9 6.3 collective-permute-start.49
  452.2 14.8 %collective-permute-start.48 = (f32[32,16]{0,1:T(8,128)S(1)}, f32[32,16]{0,1:T(8,128)S(1)}, u32[]{:S(2)}, u32[]{:S(2)}) collective-permute-start(f32[32,16]{0,1:T(8,128)S(1)} %collective-permute-done.47), channel_id=1, source_target_pairs={{0,15},{1,0},{2,1},{3,2},{4,3},{5,4},{6,5},{7,6},{8,7},{9,8},{10,9... | collective-permute-start | bytes 6152 | tf_op jit(solution)/shard_map/ppermute | solution.py:17
  461.7 5.6 collective-permute-start.50
  622.1 4.7 collective-permute-start.63
  626.8 5.8 collective-permute-start.64
  631.3 6.3 collective-permute-start.66
  632.7 14.8 %collective-permute-start.65 = (f32[32,16]{0,1:T(8,128)S(1)}, f32[32,16]{0,1:T(8,128)S(1)}, u32[]{:S(2)}, u32[]{:S(2)}) collective-permute-start(f32[32,16]{0,1:T(8,128)S(1)} %collective-permute-done.64), channel_id=1, source_target_pairs={{0,15},{1,0},{2,1},{3,2},{4,3},{5,4},{6,5},{7,6},{8,7},{9,8},{10,9... | collective-permute-start | bytes 6152 | tf_op jit(solution)/shard_map/ppermute | solution.py:17
  642.1 5.6 collective-permute-start.67
  (50 other events, 293.5 us)
Sparse Core Ops, SparseCore 0:
  46.3 111.2 all-reduce.2
  161.0 54.9 reduce-scatter.1
